TPU v7x, 128 devices: a whole 4x4x4 slice. The times are simulated.
128 devices in a mesh: cent: 4 (over y), rows: 32 (over z, x, core).
Axes of the slice: x: 4, y: 4, z: 4, core: 2. Of those that a mesh axis runs over, the one named last changes fastest.
Arguments:
- embeddings: bfloat16 [32768, 2048], P(('cent', 'rows')), may hold values from -6 to 6
- centroids: bfloat16 [16384, 2048], P(('cent', 'rows')), may hold values from -0.125 to 0.125
- cluster: int32 [32768, 1], P(('cent', 'rows')), may hold values from 0 to 127; in each aligned block of 256 rows (0 to 255, 256 to 511, ...) at most 4 rows name the same one
- noise_salt: int32 [1], replicated, may hold values from 0 to 1048575
Outputs:
- perturbed_max: float32 [32768], P(('cent', 'rows'))
- dedup_score: float32 [32768], P(('cent', 'rows'))
- new_centroids: float32 [128, 2048], P(('cent', 'rows'))
Inputs may be any that keep to these rules, and one draw needn't show every extreme that they name: In every aligned block of 256 rows (the rows of one device) no cluster is named by more than 4 rows, and in some block some cluster by exactly 4; every cluster is named by some row.
All inputs are finite; a program needn't handle non-finite values.
Results may differ from a plain program's by a relative error of at most 0.0003.
Values may be sent and summed in bfloat16 or wider, within the bound.
A program may use at most 128 MiB of HBM per device.

v0:
```python
import math
import jax
import jax.numpy as jnp
from jax import lax
from jax.sharding import PartitionSpec as P

inverse_temp = 3.0
epsilon = 1e-06


def logical_shift(word, amount):
    return lax.shift_right_logical(word, jnp.full(word.shape, amount, jnp.int32))


def gumbel_noise(row_ids, cent_ids, salt_word):
    mixed = row_ids * 1103515245 + cent_ids * 739982445 + salt_word
    mixed = mixed ^ logical_shift(mixed, 16)
    mixed = mixed * 2146121005
    mixed = mixed ^ logical_shift(mixed, 15)
    mixed = mixed * 1759714725
    mixed = mixed ^ logical_shift(mixed, 16)
    low_bits = mixed & 8388607
    uniform = (low_bits.astype(jnp.float32) + 0.5) * (1.0 / 8388608.0)
    return -jnp.log(-jnp.log(uniform))


def cluster_stats(members, valid):
    feature_dim = members.shape[1]
    widened = members.astype(jnp.float32)
    scale = lax.rsqrt(jnp.mean(widened * widened, axis=1) + epsilon)
    gram = lax.dot_general(
        members, members, (((1,), (1,)), ((), ())), preferred_element_type=jnp.float32
    )
    similar = gram * scale[:, None] * scale[None, :] * (1.0 / math.sqrt(feature_dim))
    order = jnp.arange(members.shape[0], dtype=jnp.int32)
    usable = valid[None, :] & (order[:, None] != order[None, :])
    highest = jnp.max(jnp.where(usable, similar, -1e30), axis=1)
    scores = jnp.where(jnp.any(usable, axis=1), highest, 0.0)
    total = jnp.sum(jnp.where(valid[:, None], widened, 0.0), axis=0)
    center = total * lax.rsqrt(jnp.mean(total * total) + epsilon)
    return (scores, center)


def shards(embeddings, centroids, cluster, noise_salt):
    rows_dev, feature_dim = embeddings.shape
    cent_dev = centroids.shape[0]
    cent_count = lax.axis_size("cent")
    rows_count = lax.axis_size("rows")
    devices = cent_count * rows_count
    capacity = max(2, 2 * rows_dev // devices)
    cent_index = lax.axis_index("cent")
    rows_index = lax.axis_index("rows")
    salt_word = noise_salt[0]
    group = lax.all_gather(embeddings, "cent", axis=0, tiled=True)
    position = jnp.arange(cent_count * rows_dev, dtype=jnp.int32)
    group_ids = (position // rows_dev * rows_count + rows_index) * rows_dev + position % rows_dev
    panel_base = cent_index * (rows_count * cent_dev)
    initial = jnp.full((cent_count * rows_dev,), -1e30, jnp.float32)
    piece = lax.all_gather(centroids, "rows", axis=0, tiled=True)
    piece_rows = piece.shape[0]
    block = math.gcd(piece_rows, 512)
    tiles = piece.reshape(piece_rows // block, block, feature_dim)
    offsets = jnp.arange(piece_rows // block, dtype=jnp.int32) * block

    def step(carry, item):
        tile, offset = item
        scores = lax.dot_general(
            group, tile, (((1,), (1,)), ((), ())), preferred_element_type=jnp.float32
        )
        cent_ids = panel_base + offset + jnp.arange(block, dtype=jnp.int32)
        perturbed = inverse_temp * scores + gumbel_noise(
            group_ids[:, None], cent_ids[None, :], salt_word
        )
        return (jnp.maximum(carry, jnp.max(perturbed, axis=1)), None)

    result, unused = lax.scan(step, initial, (tiles, offsets))
    merged = lax.pmax(result, "cent")
    perturbed_max = lax.dynamic_slice_in_dim(merged, cent_index * rows_dev, rows_dev)
    assigned = cluster[:, 0]
    order = jnp.arange(rows_dev, dtype=jnp.int32)
    same = (assigned[:, None] == assigned[None, :]) & (order[None, :] < order[:, None])
    rank = jnp.sum(same.astype(jnp.int32), axis=1)
    slot = assigned * capacity + rank
    outgoing = jnp.zeros((devices * capacity, feature_dim), jnp.bfloat16).at[slot].set(embeddings)
    present = (
        jnp.zeros((devices * capacity,), jnp.bfloat16)
        .at[slot]
        .set(jnp.ones((rows_dev,), jnp.bfloat16))
    )
    received, arrived = (
        lax.all_to_all(
            outgoing.reshape(devices, capacity, feature_dim),
            ("cent", "rows"),
            split_axis=0,
            concat_axis=0,
            tiled=True,
        ),
        lax.all_to_all(
            present.reshape(devices, capacity),
            ("cent", "rows"),
            split_axis=0,
            concat_axis=0,
            tiled=True,
        ),
    )
    members = received.reshape(devices * capacity, feature_dim)
    valid = arrived.reshape(devices * capacity) > 0.5
    scores, center = cluster_stats(members, valid)
    returned = lax.all_to_all(
        scores.reshape(devices, capacity), ("cent", "rows"), split_axis=0, concat_axis=0, tiled=True
    )
    dedup_score = returned.reshape(devices * capacity)[slot]
    return (perturbed_max, dedup_score, center[None, :])


def solution(mesh):
    in_specs = (
        P(("cent", "rows"), None),
        P(("cent", "rows"), None),
        P(("cent", "rows"), None),
        P(),
    )
    out_specs = (P(("cent", "rows")), P(("cent", "rows")), P(("cent", "rows"), None))
    return jax.shard_map(shards, mesh=mesh, in_specs=in_specs, out_specs=out_specs, check_vma=False)
```

profile of v0, /device:TPU:0, one launch (start us, length us, event | category | flops | bytes accessed | tf_op | source)
XLA Modules:
  0.0 242.6 jit_solution(4939791693935059020)
XLA Ops:
  7.2 0.0 all-gather.5.cloned.1.call-start
  7.2 0.7 all-gather.5.cloned.1.call-update
  7.9 0.0 all-gather.3.cloned.1.call-start
  7.9 0.7 all-gather.3.cloned.1.call-update
  8.6 0.9 convert_reduce_fusion
  9.6 0.7 compare_select_fusion
  10.3 2.2 scatter_custom_fusion
  12.4 0.8 all_to_all.17
  13.2 11.1 %all-to-all-start = ((bf16[128,1,4]{2,1,0:T(2,128)(2,1)}), bf16[128,1,4]{2,1,0:T(2,128)(2,1)S(1)}, u32[]{:S(2)}, u32[]{:S(2)}) async-start(bf16[128,1,4]{2,1,0:T(2,128)(2,1)} %all_to_all.17), calls=%async_computation | async-start | bytes 131072 | tf_op jit(solution)/shard_map/all_to_all | solution.py:98
  24.3 3.5 %scatter_custom_fusion.1 = bf16[512,2048]{1,0:T(8,128)(2,1)S(1)} fusion(s32[256]{0:T(256)S(1)} %bitcast.32, bf16[256,2048]{1,0:T(8,128)(2,1)} %param.6, bf16[]{:T(256)} %constant.99.clone.1), kind=kCustom, calls=%fused_computation.50 | custom fusion | bytes 2097664 | tf_op jit(solution)/shard_map/scatter | solution.py:84
  27.9 2.2 reshape.113
  30.1 3.5 %all-to-all-done = bf16[128,1,4]{2,1,0:T(2,128)(2,1)S(1)} async-done(((bf16[128,1,4]{2,1,0:T(2,128)(2,1)}), bf16[128,1,4]{2,1,0:T(2,128)(2,1)S(1)}, u32[]{:S(2)}, u32[]{:S(2)}) %all-to-all-start) | async-done | bytes 1056 | tf_op jit(solution)/shard_map/all_to_all | solution.py:98
  33.6 6.3 %all-to-all-start.1 = ((bf16[128,4,2048]{2,1,0:T(4,128)(2,1)}), bf16[128,4,2048]{2,1,0:T(4,128)(2,1)S(1)}, u32[]{:S(2)}, u32[]{:S(2)}) async-start(bf16[128,4,2048]{2,1,0:T(4,128)(2,1)} %reshape.113), calls=%async_computation.1 | async-start | bytes 4194304 | tf_op jit(solution)/shard_map/all_to_all | solution.py:91
  40.0 0.3 broadcast_compare_fusion
  40.2 0.1 gt.22
  40.3 0.1 copy.15
  40.4 0.1 copy.16
  40.6 0.2 fusion.41
  40.7 32.1 %all-to-all-done.1 = bf16[128,4,2048]{2,1,0:T(4,128)(2,1)S(1)} async-done(((bf16[128,4,2048]{2,1,0:T(4,128)(2,1)}), bf16[128,4,2048]{2,1,0:T(4,128)(2,1)S(1)}, u32[]{:S(2)}, u32[]{:S(2)}) %all-to-all-start.1) | async-done | bytes 2097184 | tf_op jit(solution)/shard_map/all_to_all | solution.py:91
  72.8 2.1 fusion.33
  75.0 0.1 rsqrt.18
  75.1 2.1 reshape.114
  77.1 3.6 %fusion.37 = f32[512]{0:T(512)S(1)} fusion(bf16[512,2048]{1,0:T(8,128)(2,1)} %reshape.114, f32[512]{0:T(512)S(1)} %rsqrt.18, pred[512]{0:T(512)(128)(4,1)S(1)} %gt.22), kind=kOutput, calls=%fused_computation.49 | convolution fusion | flops 1075576320 | bytes 2101760 | tf_op jit(solution)/shard_map/dot_general | solution.py:31
  80.7 0.7 select_n.51
  81.5 7.2 %all-to-all-start.2 = ((f32[128,1,4]{2,1,0:T(1,128)}), f32[128,1,4]{2,1,0:T(1,128)S(1)}, u32[]{:S(2)}, u32[]{:S(2)}) async-start(f32[128,1,4]{2,1,0:T(1,128)} %bitcast.5), calls=%async_computation.2 | async-start | bytes 131072 | tf_op jit(solution)/shard_map/all_to_all | solution.py:109
  88.7 0.6 multiply_reduce_fusion
  90.0 0.6 broadcast_multiply_fusion
  90.6 7.2 %all-to-all-done.2 = f32[128,1,4]{2,1,0:T(1,128)S(1)} async-done(((f32[128,1,4]{2,1,0:T(1,128)}), f32[128,1,4]{2,1,0:T(1,128)S(1)}, u32[]{:S(2)}, u32[]{:S(2)}) %all-to-all-start.2) | async-done | bytes 2080 | tf_op jit(solution)/shard_map/all_to_all | solution.py:109
  97.8 0.5 broadcast.166
  98.3 0.8 reduce.7
  99.2 0.1 reshape.115
  99.3 2.5 %gather_fusion = f32[256]{0:T(256)} fusion(f32[512]{0:T(512)S(1)} %reshape.115, s32[1024]{0:T(1024)S(1)} %pad_clamp_fusion), kind=kCustom, calls=%fused_computation | custom fusion | bytes 3072 | tf_op jit(solution)/shard_map/gather | solution.py:112
  101.8 0.0 all-gather.5.cloned.1.call-done
  101.8 57.1 %all-gather.3.cloned.1.call-done = bf16[4096,2048]{1,0:T(8,128)(2,1)} async-done(((bf16[128,2048]{1,0:T(8,128)(2,1)}), bf16[4096,2048]{1,0:T(8,128)(2,1)}) %all-gather.3.cloned.1.call-update) | async-done | bytes 16777232 | tf_op jit(solution)/shard_map/all_gather | solution.py:59
  158.8 65.8 %while.11 = (s32[]{:T(128)}, f32[1024]{0:T(1024)S(1)}, bf16[8,512,2048]{2,1,0:T(8,128)(2,1)}, bf16[1024,2048]{1,0:T(8,128)(2,1)}, s32[8]{0:T(128)S(1)}, /*index=...) while((s32[]{:T(128)}, f32[1024]{0:T(1024)S(1)}, bf16[8,512,2048]{2,1,0:T(8,128)(2,1)}, ...), condition=%wide.region_2.3_spmd.clone, body=%wide.region_0.2_spmd.clone.sunk | while | flops 2157464576 | bytes 6320795 | solution.py:76
  158.8 0.6 dynamic_slice.23
  160.1 6.9 %fusion.56 = f32[1024]{0:T(1024)S(1)} fusion(bf16[1024,2048]{1,0:T(8,128)(2,1)} %get-tuple-element.168, bf16[8,512,2048]{2,1,0:T(8,128)(2,1)} %get-tuple-element.167, s32[]{:T(128)S(6)} %copy.19, s32[]{:T(128)} %get-tuple-element.171, s32[512]{0:T(512)S(1)} %add_multiply_fusion.2, s32[1024]{0:T(1024)S(1)} %fusion.55), kind=kOutput, calls=%fused_computation.21.clone.1 | convolution fusion | flops 2157444096 | bytes 6302212 | tf_op jit(solution)/shard_map/while/body/eval_jaxpr/dot_general | solution.py:67
  167.0 0.6 dynamic_slice.23
  168.3 6.9 %fusion.56 = f32[1024]{0:T(1024)S(1)} fusion(bf16[1024,2048]{1,0:T(8,128)(2,1)} %get-tuple-element.168, bf16[8,512,2048]{2,1,0:T(8,128)(2,1)} %get-tuple-element.167, s32[]{:T(128)S(6)} %copy.19, s32[]{:T(128)} %get-tuple-element.171, s32[512]{0:T(512)S(1)} %add_multiply_fusion.2, s32[1024]{0:T(1024)S(1)} %fusion.55), kind=kOutput, calls=%fused_computation.21.clone.1 | convolution fusion | flops 2157444096 | bytes 6302212 | tf_op jit(solution)/shard_map/while/body/eval_jaxpr/dot_general | solution.py:67
  175.3 0.6 dynamic_slice.23
  176.5 6.9 %fusion.56 = f32[1024]{0:T(1024)S(1)} fusion(bf16[1024,2048]{1,0:T(8,128)(2,1)} %get-tuple-element.168, bf16[8,512,2048]{2,1,0:T(8,128)(2,1)} %get-tuple-element.167, s32[]{:T(128)S(6)} %copy.19, s32[]{:T(128)} %get-tuple-element.171, s32[512]{0:T(512)S(1)} %add_multiply_fusion.2, s32[1024]{0:T(1024)S(1)} %fusion.55), kind=kOutput, calls=%fused_computation.21.clone.1 | convolution fusion | flops 2157444096 | bytes 6302212 | tf_op jit(solution)/shard_map/while/body/eval_jaxpr/dot_general | solution.py:67
  183.5 0.6 dynamic_slice.23
  184.8 6.9 %fusion.56 = f32[1024]{0:T(1024)S(1)} fusion(bf16[1024,2048]{1,0:T(8,128)(2,1)} %get-tuple-element.168, bf16[8,512,2048]{2,1,0:T(8,128)(2,1)} %get-tuple-element.167, s32[]{:T(128)S(6)} %copy.19, s32[]{:T(128)} %get-tuple-element.171, s32[512]{0:T(512)S(1)} %add_multiply_fusion.2, s32[1024]{0:T(1024)S(1)} %fusion.55), kind=kOutput, calls=%fused_computation.21.clone.1 | convolution fusion | flops 2157444096 | bytes 6302212 | tf_op jit(solution)/shard_map/while/body/eval_jaxpr/dot_general | solution.py:67
  191.7 0.6 dynamic_slice.23
  193.0 6.9 %fusion.56 = f32[1024]{0:T(1024)S(1)} fusion(bf16[1024,2048]{1,0:T(8,128)(2,1)} %get-tuple-element.168, bf16[8,512,2048]{2,1,0:T(8,128)(2,1)} %get-tuple-element.167, s32[]{:T(128)S(6)} %copy.19, s32[]{:T(128)} %get-tuple-element.171, s32[512]{0:T(512)S(1)} %add_multiply_fusion.2, s32[1024]{0:T(1024)S(1)} %fusion.55), kind=kOutput, calls=%fused_computation.21.clone.1 | convolution fusion | flops 2157444096 | bytes 6302212 | tf_op jit(solution)/shard_map/while/body/eval_jaxpr/dot_general | solution.py:67
  200.0 0.6 dynamic_slice.23
  201.2 6.9 %fusion.56 = f32[1024]{0:T(1024)S(1)} fusion(bf16[1024,2048]{1,0:T(8,128)(2,1)} %get-tuple-element.168, bf16[8,512,2048]{2,1,0:T(8,128)(2,1)} %get-tuple-element.167, s32[]{:T(128)S(6)} %copy.19, s32[]{:T(128)} %get-tuple-element.171, s32[512]{0:T(512)S(1)} %add_multiply_fusion.2, s32[1024]{0:T(1024)S(1)} %fusion.55), kind=kOutput, calls=%fused_computation.21.clone.1 | convolution fusion | flops 2157444096 | bytes 6302212 | tf_op jit(solution)/shard_map/while/body/eval_jaxpr/dot_general | solution.py:67
  208.2 0.6 dynamic_slice.23
  209.4 6.9 %fusion.56 = f32[1024]{0:T(1024)S(1)} fusion(bf16[1024,2048]{1,0:T(8,128)(2,1)} %get-tuple-element.168, bf16[8,512,2048]{2,1,0:T(8,128)(2,1)} %get-tuple-element.167, s32[]{:T(128)S(6)} %copy.19, s32[]{:T(128)} %get-tuple-element.171, s32[512]{0:T(512)S(1)} %add_multiply_fusion.2, s32[1024]{0:T(1024)S(1)} %fusion.55), kind=kOutput, calls=%fused_computation.21.clone.1 | convolution fusion | flops 2157444096 | bytes 6302212 | tf_op jit(solution)/shard_map/while/body/eval_jaxpr/dot_general | solution.py:67
  216.4 0.6 dynamic_slice.23
  217.7 6.9 %fusion.56 = f32[1024]{0:T(1024)S(1)} fusion(bf16[1024,2048]{1,0:T(8,128)(2,1)} %get-tuple-element.168, bf16[8,512,2048]{2,1,0:T(8,128)(2,1)} %get-tuple-element.167, s32[]{:T(128)S(6)} %copy.19, s32[]{:T(128)} %get-tuple-element.171, s32[512]{0:T(512)S(1)} %add_multiply_fusion.2, s32[1024]{0:T(1024)S(1)} %fusion.55), kind=kOutput, calls=%fused_computation.21.clone.1 | convolution fusion | flops 2157444096 | bytes 6302212 | tf_op jit(solution)/shard_map/while/body/eval_jaxpr/dot_general | solution.py:67
  224.6 10.5 %pmax.7 = f32[1024]{0:T(1024)S(1)} all-reduce(f32[1024]{0:T(1024)S(1)} %get-tuple-element.45), channel_id=1, replica_groups=mesh['cent'=4,'rows'=32] {'cent'}, use_global_device_ids=true, to_apply=%region_3.4 | all-reduce | flops 1024 | bytes 8192 | tf_op jit(solution)/shard_map/pmax | solution.py:77
  235.1 0.6 dynamic_slice.11
  (30 shorter events, 0.2 us)
Async XLA Ops:
  7.2 94.6 %all-gather.5.cloned.1.call-start = ((), (), s32[]{:S(2)}) async-start(), calls=%async_computation.4 | async-start | bytes 5242880 | tf_op jit(solution)/shard_map/all_gather | solution.py:54
  7.9 150.9 %all-gather.3.cloned.1.call-start = ((), (), s32[]{:S(2)}) async-start(), calls=%async_computation.3 | async-start | bytes 17301504 | tf_op jit(solution)/shard_map/all_gather | solution.py:59
  13.2 20.4 %all-to-all-start = ((bf16[128,1,4]{2,1,0:T(2,128)(2,1)}), bf16[128,1,4]{2,1,0:T(2,128)(2,1)S(1)}, u32[]{:S(2)}, u32[]{:S(2)}) async-start(bf16[128,1,4]{2,1,0:T(2,128)(2,1)} %all_to_all.17), calls=%async_computation | async-start | bytes 131072 | tf_op jit(solution)/shard_map/all_to_all | solution.py:98
  33.6 39.2 %all-to-all-start.1 = ((bf16[128,4,2048]{2,1,0:T(4,128)(2,1)}), bf16[128,4,2048]{2,1,0:T(4,128)(2,1)S(1)}, u32[]{:S(2)}, u32[]{:S(2)}) async-start(bf16[128,4,2048]{2,1,0:T(4,128)(2,1)} %reshape.113), calls=%async_computation.1 | async-start | bytes 4194304 | tf_op jit(solution)/shard_map/all_to_all | solution.py:91
  81.5 16.3 %all-to-all-start.2 = ((f32[128,1,4]{2,1,0:T(1,128)}), f32[128,1,4]{2,1,0:T(1,128)S(1)}, u32[]{:S(2)}, u32[]{:S(2)}) async-start(f32[128,1,4]{2,1,0:T(1,128)} %bitcast.5), calls=%async_computation.2 | async-start | bytes 131072 | tf_op jit(solution)/shard_map/all_to_all | solution.py:109
Sparse Core Ops, SparseCore 0:
  9.7 73.9 all-gather.4
  85.9 72.9 all-gather.2
where the time goes:
time: 243 us
  waiting for transfers between devices  101 us (42%)
  matrix products  59 us (24%)
  starting transfers between devices  24.7 us (10%)
  local copies, waits for them, and re-layouts  20.6 us (8%)
  between operations  14.9 us (6%)
  blocking collectives  10.5 us (4%)
  other arithmetic  6.36 us (3%)
  loops' own time  5.28 us (2%)
    all_gather x1, waiting for transfers between devices, shards(): piece = lax.all_gather(centroids, 'rows', axis=0, tiled=True)  57.1 us
    dot_general x8, matrix products, step(): lax.dot_general(group, tile, (((1,), (1,)), ((), ())), preferred_element_...  55.4 us
    all_to_all x1, waiting for transfers between devices, shards(): lax.all_to_all(outgoing.reshape(devices, capacity, feature_dim), ('cent',...  32.1 us
    all_to_all x1, starting transfers between devices, shards(): lax.all_to_all(present.reshape(devices, capacity), ('cent', 'rows'), spli...  11.1 us
    pmax x1, blocking collectives, shards(): merged = lax.pmax(result, 'cent')  10.5 us
    all_to_all x1, waiting for transfers between devices, shards(): lax.all_to_all(scores.reshape(devices, capacity), ('cent', 'rows'), split...  7.23 us
    all_to_all x1, starting transfers between devices, shards(): lax.all_to_all(scores.reshape(devices, capacity), ('cent', 'rows'), split...  7.22 us
    all_to_all x1, starting transfers between devices, shards(): lax.all_to_all(outgoing.reshape(devices, capacity, feature_dim), ('cent',...  6.27 us
  transfers between devices with their start and end apart: 5, of which 4 were waited for; matrix products, arithmetic and copies ran while one was open for 10% of the time, Pallas kernels for 0%

commit v1 on v0

--- a/solution.py
+++ b/solution.py
@@ -56,7 +56,9 @@
     group_ids = (position // rows_dev * rows_count + rows_index) * rows_dev + position % rows_dev
     panel_base = cent_index * (rows_count * cent_dev)
     initial = jnp.full((cent_count * rows_dev,), -1e30, jnp.float32)
-    piece = lax.all_gather(centroids, "rows", axis=0, tiled=True)
+    piece = jnp.concatenate(
+        lax.all_to_all(jnp.stack([centroids] * lax.axis_size("rows")), "rows", 0, 0), axis=0
+    )
     piece_rows = piece.shape[0]
     block = math.gcd(piece_rows, 512)
     tiles = piece.reshape(piece_rows // block, block, feature_dim)

time: 243 us -> 397 us (1.63)
  waiting for transfers between devices: 101 us -> 240 us
  blocking collectives: 10.5 us -> 22.4 us
  local copies, waits for them, and re-layouts: 20.6 us -> 25.7 us
    all_to_all x1, waiting for transfers between devices: 7.23 us -> 163 us  [shards(): lax.all_to_all(jnp.stack([centroids] * lax.axis_size('rows')), 'rows', 0, 0)]
    all_gather x1 -> x0, waiting for transfers between devices: 57.1 us -> none  [shards(): piece = lax.all_gather(centroids, 'rows', axis=0, tiled=True)]
    all_gather x1, waiting for transfers between devices: 0.01 us -> 43.7 us  [shards(): group = lax.all_gather(embeddings, 'cent', axis=0, tiled=True)]
    all_to_all x0 -> x1, blocking collectives: none -> 13.6 us  [shards(): lax.all_to_all(scores.reshape(devices, capacity), ('cent', 'rows'), split...]
    another operation x0 -> x1, local copies, waits for them, and re-layouts: none -> 5.94 us  [shards(): jnp.stack([centroids] * lax.axis_size('rows'))]
  transfers between devices with their start and end apart: 5 -> 4, of which waited for: 4 -> 4; matrix products, arithmetic and copies ran while one was open for 10% -> 3% of each run, Pallas kernels for 0% -> 0%
where the time goes in v1:
time: 397 us; the launch traced here: 396 us
  waiting for transfers between devices  240 us (60%)
  matrix products  59.1 us (15%)
  local copies, waits for them, and re-layouts  25.7 us (6%)
  starting transfers between devices  22.7 us (6%)
  blocking collectives  22.4 us (6%)
  between operations  14.9 us (4%)
  other arithmetic  6.35 us (2%)
  loops' own time  4.89 us (1%)
    all_to_all x1, waiting for transfers between devices, shards(): lax.all_to_all(jnp.stack([centroids] * lax.axis_size('rows')), 'rows', 0, 0)  163 us
    dot_general x8, matrix products, step(): lax.dot_general(group, tile, (((1,), (1,)), ((), ())), preferred_element_...  55.4 us
    all_gather x1, waiting for transfers between devices, shards(): group = lax.all_gather(embeddings, 'cent', axis=0, tiled=True)  43.7 us
    all_to_all x1, waiting for transfers between devices, shards(): lax.all_to_all(outgoing.reshape(devices, capacity, feature_dim), ('cent',...  29.6 us
    all_to_all x1, blocking collectives, shards(): lax.all_to_all(scores.reshape(devices, capacity), ('cent', 'rows'), split...  13.6 us
    all_to_all x1, starting transfers between devices, shards(): lax.all_to_all(present.reshape(devices, capacity), ('cent', 'rows'), spli...  11.1 us
    pmax x1, blocking collectives, shards(): merged = lax.pmax(result, 'cent')  8.8 us
  transfers between devices with their start and end apart: 4, of which 4 were waited for; matrix products, arithmetic and copies ran while one was open for 3% of the time, Pallas kernels for 0%

profile of v1, /device:TPU:0, one launch (start us, length us, event | category | flops | bytes accessed | tf_op | source)
XLA Modules:
  0.0 396.3 jit_solution(1367589415131992252)
XLA Ops:
  7.2 0.9 convert_reduce_fusion
  8.1 0.7 compare_select_fusion
  8.8 2.2 scatter_custom_fusion
  11.0 0.8 all_to_all.21
  11.7 11.1 %all-to-all-start.1 = ((bf16[128,1,4]{2,1,0:T(2,128)(2,1)}), bf16[128,1,4]{2,1,0:T(2,128)(2,1)S(1)}, u32[]{:S(2)}, u32[]{:S(2)}) async-start(bf16[128,1,4]{2,1,0:T(2,128)(2,1)} %all_to_all.21), calls=%async_computation.1 | async-start | bytes 131072 | tf_op jit(solution)/shard_map/all_to_all | solution.py:100
  22.9 3.5 scatter_custom_fusion.1
  26.4 2.2 reshape.111
  28.6 3.6 all-to-all-done.1
  32.2 6.2 %all-to-all-start.2 = ((bf16[128,4,2048]{2,1,0:T(4,128)(2,1)}), bf16[128,4,2048]{2,1,0:T(4,128)(2,1)S(1)}, u32[]{:S(2)}, u32[]{:S(2)}) async-start(bf16[128,4,2048]{2,1,0:T(4,128)(2,1)} %reshape.111), calls=%async_computation.2 | async-start | bytes 4194304 | tf_op jit(solution)/shard_map/all_to_all | solution.py:93
  38.4 0.3 broadcast_compare_fusion
  38.6 0.1 gt.22
  38.8 0.1 copy.15
  38.9 0.1 copy.16
  39.0 0.2 fusion.41
  39.2 29.6 %all-to-all-done.2 = bf16[128,4,2048]{2,1,0:T(4,128)(2,1)S(1)} async-done(((bf16[128,4,2048]{2,1,0:T(4,128)(2,1)}), bf16[128,4,2048]{2,1,0:T(4,128)(2,1)S(1)}, u32[]{:S(2)}, u32[]{:S(2)}) %all-to-all-start.2) | async-done | bytes 2097184 | tf_op jit(solution)/shard_map/all_to_all | solution.py:93
  68.8 2.1 fusion.33
  70.9 0.1 rsqrt.18
  71.0 2.1 reshape.112
  73.1 0.0 copy-start
  73.1 3.7 fusion.37
  76.8 0.1 select_n.51
  76.9 13.6 %all_to_all.26 = f32[128,1,4]{2,1,0:T(1,128)S(1)} all-to-all(f32[128,1,4]{2,1,0:T(1,128)S(1)} %bitcast.29), channel_id=1, replica_groups=mesh['cent'=4,'rows'=32] {'cent','rows'}, dimensions={0} | all-to-all | bytes 4096 | tf_op jit(solution)/shard_map/all_to_all | solution.py:111
  90.5 0.0 copy-done
  90.5 5.9 %stack.2 = bf16[32,128,2048]{2,1,0:T(8,128)(2,1)} broadcast(bf16[128,2048]{1,0:T(8,128)(2,1)S(1)} %copy-done), dimensions={1,2} | broadcast | bytes 17301504 | tf_op jit(solution)/shard_map/stack | solution.py:60
  96.5 5.2 %all-to-all-start = ((bf16[32,128,2048]{2,1,0:T(8,128)(2,1)}), bf16[32,128,2048]{2,1,0:T(8,128)(2,1)}, u32[]{:S(2)}, u32[]{:S(2)}) async-start(bf16[32,128,2048]{2,1,0:T(8,128)(2,1)} %stack.2), calls=%async_computation | async-start | bytes 33554432 | tf_op jit(solution)/shard_map/all_to_all | solution.py:60
  101.6 0.2 all-gather.2.cloned.1.call-start
  101.9 0.5 all-gather.2.cloned.1.call-update
  102.4 0.6 multiply_reduce_fusion
  103.7 0.6 broadcast_multiply_fusion
  104.3 0.5 broadcast.168
  104.8 0.8 reduce.7
  105.6 0.1 reshape.113
  105.7 2.5 gather_fusion
  108.2 43.7 %all-gather.2.cloned.1.call-done = bf16[1024,2048]{1,0:T(8,128)(2,1)} async-done(((bf16[256,2048]{1,0:T(8,128)(2,1)}), bf16[1024,2048]{1,0:T(8,128)(2,1)}) %all-gather.2.cloned.1.call-update) | async-done | bytes 4194320 | tf_op jit(solution)/shard_map/all_gather | solution.py:54
  151.9 162.9 %all-to-all-done = bf16[32,128,2048]{2,1,0:T(8,128)(2,1)} async-done(((bf16[32,128,2048]{2,1,0:T(8,128)(2,1)}), bf16[32,128,2048]{2,1,0:T(8,128)(2,1)}, u32[]{:S(2)}, u32[]{:S(2)}) %all-to-all-start) | async-done | bytes 16777248 | tf_op jit(solution)/shard_map/all_to_all | solution.py:60
  314.9 65.1 %while.11 = (s32[]{:T(128)}, f32[1024]{0:T(1024)S(1)}, bf16[8,512,2048]{2,1,0:T(8,128)(2,1)}, bf16[1024,2048]{1,0:T(8,128)(2,1)}, s32[8]{0:T(128)S(1)}, /*index=...) while((s32[]{:T(128)}, f32[1024]{0:T(1024)S(1)}, bf16[8,512,2048]{2,1,0:T(8,128)(2,1)}, ...), condition=%wide.region_2.3_spmd.clone, body=%wide.region_0.2_spmd.clone.sunk | while | flops 2157464576 | bytes 6320795 | solution.py:78
  314.9 0.6 dynamic_slice.23
  316.0 6.9 %fusion.56 = f32[1024]{0:T(1024)S(1)} fusion(bf16[1024,2048]{1,0:T(8,128)(2,1)} %get-tuple-element.168, bf16[8,512,2048]{2,1,0:T(8,128)(2,1)} %get-tuple-element.167, s32[]{:T(128)S(6)} %copy.19, s32[]{:T(128)} %get-tuple-element.171, s32[512]{0:T(512)S(1)} %add_multiply_fusion.2, s32[1024]{0:T(1024)S(1)} %fusion.55), kind=kOutput, calls=%fused_computation.21.clone.1 | convolution fusion | flops 2157444096 | bytes 6302212 | tf_op jit(solution)/shard_map/while/body/eval_jaxpr/dot_general | solution.py:69
  323.0 0.6 dynamic_slice.23
  324.2 6.9 %fusion.56 = f32[1024]{0:T(1024)S(1)} fusion(bf16[1024,2048]{1,0:T(8,128)(2,1)} %get-tuple-element.168, bf16[8,512,2048]{2,1,0:T(8,128)(2,1)} %get-tuple-element.167, s32[]{:T(128)S(6)} %copy.19, s32[]{:T(128)} %get-tuple-element.171, s32[512]{0:T(512)S(1)} %add_multiply_fusion.2, s32[1024]{0:T(1024)S(1)} %fusion.55), kind=kOutput, calls=%fused_computation.21.clone.1 | convolution fusion | flops 2157444096 | bytes 6302212 | tf_op jit(solution)/shard_map/while/body/eval_jaxpr/dot_general | solution.py:69
  331.2 0.6 dynamic_slice.23
  332.3 6.9 %fusion.56 = f32[1024]{0:T(1024)S(1)} fusion(bf16[1024,2048]{1,0:T(8,128)(2,1)} %get-tuple-element.168, bf16[8,512,2048]{2,1,0:T(8,128)(2,1)} %get-tuple-element.167, s32[]{:T(128)S(6)} %copy.19, s32[]{:T(128)} %get-tuple-element.171, s32[512]{0:T(512)S(1)} %add_multiply_fusion.2, s32[1024]{0:T(1024)S(1)} %fusion.55), kind=kOutput, calls=%fused_computation.21.clone.1 | convolution fusion | flops 2157444096 | bytes 6302212 | tf_op jit(solution)/shard_map/while/body/eval_jaxpr/dot_general | solution.py:69
  339.3 0.6 dynamic_slice.23
  340.5 6.9 %fusion.56 = f32[1024]{0:T(1024)S(1)} fusion(bf16[1024,2048]{1,0:T(8,128)(2,1)} %get-tuple-element.168, bf16[8,512,2048]{2,1,0:T(8,128)(2,1)} %get-tuple-element.167, s32[]{:T(128)S(6)} %copy.19, s32[]{:T(128)} %get-tuple-element.171, s32[512]{0:T(512)S(1)} %add_multiply_fusion.2, s32[1024]{0:T(1024)S(1)} %fusion.55), kind=kOutput, calls=%fused_computation.21.clone.1 | convolution fusion | flops 2157444096 | bytes 6302212 | tf_op jit(solution)/shard_map/while/body/eval_jaxpr/dot_general | solution.py:69
  347.4 0.6 dynamic_slice.23
  348.6 6.9 %fusion.56 = f32[1024]{0:T(1024)S(1)} fusion(bf16[1024,2048]{1,0:T(8,128)(2,1)} %get-tuple-element.168, bf16[8,512,2048]{2,1,0:T(8,128)(2,1)} %get-tuple-element.167, s32[]{:T(128)S(6)} %copy.19, s32[]{:T(128)} %get-tuple-element.171, s32[512]{0:T(512)S(1)} %add_multiply_fusion.2, s32[1024]{0:T(1024)S(1)} %fusion.55), kind=kOutput, calls=%fused_computation.21.clone.1 | convolution fusion | flops 2157444096 | bytes 6302212 | tf_op jit(solution)/shard_map/while/body/eval_jaxpr/dot_general | solution.py:69
  355.6 0.6 dynamic_slice.23
  356.8 6.9 %fusion.56 = f32[1024]{0:T(1024)S(1)} fusion(bf16[1024,2048]{1,0:T(8,128)(2,1)} %get-tuple-element.168, bf16[8,512,2048]{2,1,0:T(8,128)(2,1)} %get-tuple-element.167, s32[]{:T(128)S(6)} %copy.19, s32[]{:T(128)} %get-tuple-element.171, s32[512]{0:T(512)S(1)} %add_multiply_fusion.2, s32[1024]{0:T(1024)S(1)} %fusion.55), kind=kOutput, calls=%fused_computation.21.clone.1 | convolution fusion | flops 2157444096 | bytes 6302212 | tf_op jit(solution)/shard_map/while/body/eval_jaxpr/dot_general | solution.py:69
  363.7 0.6 dynamic_slice.23
  364.9 6.9 %fusion.56 = f32[1024]{0:T(1024)S(1)} fusion(bf16[1024,2048]{1,0:T(8,128)(2,1)} %get-tuple-element.168, bf16[8,512,2048]{2,1,0:T(8,128)(2,1)} %get-tuple-element.167, s32[]{:T(128)S(6)} %copy.19, s32[]{:T(128)} %get-tuple-element.171, s32[512]{0:T(512)S(1)} %add_multiply_fusion.2, s32[1024]{0:T(1024)S(1)} %fusion.55), kind=kOutput, calls=%fused_computation.21.clone.1 | convolution fusion | flops 2157444096 | bytes 6302212 | tf_op jit(solution)/shard_map/while/body/eval_jaxpr/dot_general | solution.py:69
  371.9 0.6 dynamic_slice.23
  373.0 6.9 %fusion.56 = f32[1024]{0:T(1024)S(1)} fusion(bf16[1024,2048]{1,0:T(8,128)(2,1)} %get-tuple-element.168, bf16[8,512,2048]{2,1,0:T(8,128)(2,1)} %get-tuple-element.167, s32[]{:T(128)S(6)} %copy.19, s32[]{:T(128)} %get-tuple-element.171, s32[512]{0:T(512)S(1)} %add_multiply_fusion.2, s32[1024]{0:T(1024)S(1)} %fusion.55), kind=kOutput, calls=%fused_computation.21.clone.1 | convolution fusion | flops 2157444096 | bytes 6302212 | tf_op jit(solution)/shard_map/while/body/eval_jaxpr/dot_general | solution.py:69
  380.0 8.8 %pmax.7 = f32[1024]{0:T(1024)S(1)} all-reduce(f32[1024]{0:T(1024)S(1)} %get-tuple-element.45), channel_id=1, replica_groups=mesh['cent'=4,'rows'=32] {'cent'}, use_global_device_ids=true, to_apply=%region_3.4 | all-reduce | flops 1024 | bytes 8192 | tf_op jit(solution)/shard_map/pmax | solution.py:79
  388.8 0.6 dynamic_slice.11
  (30 shorter events, 0.2 us)
Async XLA Ops:
  11.7 20.4 %all-to-all-start.1 = ((bf16[128,1,4]{2,1,0:T(2,128)(2,1)}), bf16[128,1,4]{2,1,0:T(2,128)(2,1)S(1)}, u32[]{:S(2)}, u32[]{:S(2)}) async-start(bf16[128,1,4]{2,1,0:T(2,128)(2,1)} %all_to_all.21), calls=%async_computation.1 | async-start | bytes 131072 | tf_op jit(solution)/shard_map/all_to_all | solution.py:100
  32.2 36.6 %all-to-all-start.2 = ((bf16[128,4,2048]{2,1,0:T(4,128)(2,1)}), bf16[128,4,2048]{2,1,0:T(4,128)(2,1)S(1)}, u32[]{:S(2)}, u32[]{:S(2)}) async-start(bf16[128,4,2048]{2,1,0:T(4,128)(2,1)} %reshape.111), calls=%async_computation.2 | async-start | bytes 4194304 | tf_op jit(solution)/shard_map/all_to_all | solution.py:93
  73.1 17.4 %copy-start = (bf16[128,2048]{1,0:T(8,128)(2,1)S(1)}, bf16[128,2048]{1,0:T(8,128)(2,1)}, u32[]{:S(2)}) copy-start(bf16[128,2048]{1,0:T(8,128)(2,1)} %param.7) | copy-start | bytes 1572868
  96.5 218.4 %all-to-all-start = ((bf16[32,128,2048]{2,1,0:T(8,128)(2,1)}), bf16[32,128,2048]{2,1,0:T(8,128)(2,1)}, u32[]{:S(2)}, u32[]{:S(2)}) async-start(bf16[32,128,2048]{2,1,0:T(8,128)(2,1)} %stack.2), calls=%async_computation | async-start | bytes 33554432 | tf_op jit(solution)/shard_map/all_to_all | solution.py:60
  101.6 50.3 %all-gather.2.cloned.1.call-start = ((), (), s32[]{:S(2)}) async-start(), calls=%async_computation.4 | async-start | bytes 5242880 | tf_op jit(solution)/shard_map/all_gather | solution.py:54
Sparse Core Ops, SparseCore 0:
  104.1 47.7 all-gather.1
